TPU v7x, 256 devices: a whole 4x4x8 slice. The times are simulated.
256 devices in a mesh: row: 8 (over x, core), col: 32 (over z, y).
Axes of the slice: x: 4, y: 4, z: 8, core: 2. Of those that a mesh axis runs over, the one named last changes fastest.
Arguments:
- matrix: float32 [24576, 12288], P('row', 'col'), may hold values from -6 to 6
Outputs:
- updated: float32 [24576, 12288], P('row', 'col')
All inputs are finite; a program needn't handle non-finite values.
Results may differ from a plain program's by a relative error of at most 0.0003.
Values sent between devices are 32-bit elements; how exact they have to be, the bound alone decides.
A program may use at most 64 MiB of HBM per device.

v0:
```python
import jax
import jax.numpy as jnp
from jax import lax
from jax.sharding import PartitionSpec as P

PANEL = 256
HIGHEST = lax.Precision.HIGHEST


def partner_2(block, axis, distance):
    count = lax.axis_size(axis)
    route = []
    for low in range(count):
        high = low | 1 << distance
        if high != low and high < count:
            route += [(low, high), (high, low)]
    return lax.ppermute(block, axis, route)


def broadcast(value, axis, source):
    kept = jnp.where(lax.axis_index(axis) == source, value, 0).astype(value.dtype)
    return lax.psum(kept, axis)


def upper_of(gram):
    return jnp.linalg.cholesky(gram).T


def combine_pair(upper_one, upper_two):
    gram = jnp.dot(upper_one.T, upper_one, precision=HIGHEST) + jnp.dot(
        upper_two.T, upper_two, precision=HIGHEST
    )
    return upper_of(gram)


def apply_inverse(upper, rows):
    return jax.scipy.linalg.solve_triangular(upper.T, rows.T, lower=True).T


def factor(panel):
    gram_local = lax.dot_general(panel, panel, (((0,), (0,)), ((), ())), precision=HIGHEST)
    is_first = lax.axis_index("row") == 0
    identity = jnp.eye(PANEL, dtype=jnp.float32)
    upper = upper_of(gram_local)
    for level in range(lax.axis_size("row").bit_length() - 1):
        partner = partner_2(upper, "row", level)
        upper = combine_pair(upper, partner)
    basis = apply_inverse(upper, panel)
    top_block = broadcast(basis[:PANEL], "row", 0)
    lead = identity + top_block
    vectors = basis.at[:PANEL].add(jnp.where(is_first, identity, jnp.zeros_like(identity)))
    return (vectors, lead)


def on_device(matrix):
    panel = matrix[:, :PANEL]
    vectors, lead = factor(panel)
    vectors, lead = (broadcast(vectors, "col", 0), broadcast(lead, "col", 0))
    partial_proj = lax.dot_general(vectors, matrix, (((0,), (0,)), ((), ())), precision=HIGHEST)
    projected = lax.psum(partial_proj, "row")
    lead_gram = jnp.dot(lead.T, lead, precision=HIGHEST)
    lead_factor = jnp.linalg.cholesky(lead_gram)
    coeffs = jax.scipy.linalg.cho_solve(
        (lead_factor, True), jnp.dot(lead.T, projected, precision=HIGHEST)
    )
    return matrix - jnp.dot(vectors, coeffs, precision=HIGHEST)


def solution(mesh):
    in_specs = (P("row", "col"),)
    out_specs = P("row", "col")
    return jax.shard_map(
        on_device, mesh=mesh, in_specs=in_specs, out_specs=out_specs, check_vma=False
    )
```

profile of v0, /device:TPU:8, one launch (start us, length us, event | category | flops | bytes accessed | tf_op | source)
XLA Modules:
  0.0 583.5 jit_solution(9986484635231155321)
XLA Ops:
  6.5 7.9 %fusion.1 = f32[256,256]{1,0:T(8,128)S(1)} fusion(f32[3072,384]{1,0:T(8,128)} %param.4), kind=kOutput, calls=%fused_computation.11 | convolution fusion | flops 2415919104 | bytes 3407872 | tf_op jit(solution)/shard_map/dot_general | solution.py:41
  14.7 11.7 %cholesky.256 = f32[128,128]{1,0:T(8,128)S(1)} custom-call(f32[128,128]{1,0:T(8,128)S(1)} %cholesky.422), custom_call_target="Cholesky" | custom-call | tf_op jit(solution)/shard_map/jit(cholesky)/cholesky | solution.py:26
  26.4 9.8 %custom-call.25 = f32[1,128,128]{1,2,0:T(8,128)S(1)} custom-call(f32[1,128,128]{2,1,0:T(8,128)S(1)} %get-tuple-element.77), custom_call_target="InvertDiagBlocksLowerTriangular" | custom-call | tf_op jit(solution)/shard_map/jit(cholesky)/cholesky | solution.py:26
  36.8 11.9 %cholesky.273 = f32[128,128]{1,0:T(8,128)S(1)} custom-call(f32[128,128]{1,0:T(8,128)S(1)} %convolution_subtract_fusion.5), custom_call_target="Cholesky" | custom-call | tf_op jit(solution)/shard_map/jit(cholesky)/cholesky | solution.py:26
  48.7 0.7 compare_reduce_fusion.8
  51.3 1.1 collective-permute-done
  53.0 11.7 %cholesky.290 = f32[128,128]{1,0:T(8,128)S(1)} custom-call(f32[128,128]{1,0:T(8,128)S(1)} %cholesky.425), custom_call_target="Cholesky" | custom-call | tf_op jit(solution)/shard_map/jit(cholesky)/cholesky | solution.py:26
  64.8 9.8 %custom-call.26 = f32[1,128,128]{1,2,0:T(8,128)S(1)} custom-call(f32[1,128,128]{2,1,0:T(8,128)S(1)} %get-tuple-element.73), custom_call_target="InvertDiagBlocksLowerTriangular" | custom-call | tf_op jit(solution)/shard_map/jit(cholesky)/cholesky | solution.py:26
  75.1 11.7 %cholesky.307 = f32[128,128]{1,0:T(8,128)S(1)} custom-call(f32[128,128]{1,0:T(8,128)S(1)} %slice_subtract_fusion.2), custom_call_target="Cholesky" | custom-call | tf_op jit(solution)/shard_map/jit(cholesky)/cholesky | solution.py:26
  86.8 0.7 compare_reduce_fusion.6
  87.6 0.6 compare_reduce_fusion.7
  89.6 2.0 collective-permute-start.1
  91.6 3.8 slice_bitcast_fusion
  95.7 2.7 collective-permute-done.1
  99.0 11.7 %cholesky.324 = f32[128,128]{1,0:T(8,128)S(1)} custom-call(f32[128,128]{1,0:T(8,128)S(1)} %cholesky.428), custom_call_target="Cholesky" | custom-call | tf_op jit(solution)/shard_map/jit(cholesky)/cholesky | solution.py:26
  110.8 9.8 %custom-call.27 = f32[1,128,128]{1,2,0:T(8,128)S(1)} custom-call(f32[1,128,128]{2,1,0:T(8,128)S(1)} %get-tuple-element.69), custom_call_target="InvertDiagBlocksLowerTriangular" | custom-call | tf_op jit(solution)/shard_map/jit(cholesky)/cholesky | solution.py:26
  121.1 11.7 %cholesky.341 = f32[128,128]{1,0:T(8,128)S(1)} custom-call(f32[128,128]{1,0:T(8,128)S(1)} %slice_subtract_fusion.1), custom_call_target="Cholesky" | custom-call | tf_op jit(solution)/shard_map/jit(cholesky)/cholesky | solution.py:26
  132.8 0.6 compare_reduce_fusion.4
  133.5 0.7 compare_reduce_fusion.5
  135.5 3.3 collective-permute-start.2
  139.2 5.6 collective-permute-done.2
  145.3 11.7 %cholesky.358 = f32[128,128]{1,0:T(8,128)S(1)} custom-call(f32[128,128]{1,0:T(8,128)S(1)} %cholesky.431), custom_call_target="Cholesky" | custom-call | tf_op jit(solution)/shard_map/jit(cholesky)/cholesky | solution.py:26
  157.1 9.8 %custom-call.28 = f32[1,128,128]{1,2,0:T(8,128)S(1)} custom-call(f32[1,128,128]{2,1,0:T(8,128)S(1)} %get-tuple-element.65), custom_call_target="InvertDiagBlocksLowerTriangular" | custom-call | tf_op jit(solution)/shard_map/jit(cholesky)/cholesky | solution.py:26
  167.4 11.7 %cholesky.375 = f32[128,128]{1,0:T(8,128)S(1)} custom-call(f32[128,128]{1,0:T(8,128)S(1)} %slice_subtract_fusion), custom_call_target="Cholesky" | custom-call | tf_op jit(solution)/shard_map/jit(cholesky)/cholesky | solution.py:26
  179.2 0.7 compare_reduce_fusion.2
  179.8 0.6 compare_reduce_fusion.3
  181.8 4.0 while.3
  182.6 1.3 bitcast_dynamic-update-slice_fusion.4
  184.5 1.3 bitcast_dynamic-update-slice_fusion.4
  185.8 19.7 %custom-call.19 = f32[2,128,128]{1,2,0:T(8,128)S(1)} custom-call(f32[2,128,128]{2,1,0:T(8,128)S(1)} %get-tuple-element.25), custom_call_target="InvertDiagBlocksLowerTriangular" | custom-call | tf_op jit(solution)/shard_map/jit(_solve_triangular)/triangular_solve | solution.py:37
  205.5 2.9 fusion.3
  208.4 5.2 convolution_subtract_fusion.1
  214.0 2.8 fusion.38
  217.1 0.8 slice_select_fusion
  217.9 1.7 copy-done
  219.6 1.9 broadcast_select_fusion
  221.5 66.5 %all-reduce.6.cloned.1.call-done = f32[256,256]{1,0:T(8,128)} async-done(((f32[256,256]{1,0:T(8,128)}), f32[256,256]{1,0:T(8,128)}) %all-reduce.6.cloned.1.call-update) | async-done | bytes 262160 | tf_op jit(solution)/shard_map/psum | solution.py:22
  287.9 1.7 fusion.10
  290.1 159.1 %all-reduce.10.cloned.1.call-done = (f32[3072,256]{1,0:T(8,128)}, f32[256,256]{1,0:T(8,128)}) async-done(((f32[3072,256]{1,0:T(8,128)}, f32[256,256]{1,0:T(8,128)}), (f32[3072,256]{1,0:T(8,128)}, f32[256,256]{1,0:T(8,128)})) %all-reduce.10.cloned.1.call-update) | async-done | bytes 3407888 | tf_op jit(solution)/shard_map/psum | solution.py:22
  449.2 1.8 fusion.78
  451.0 0.8 copy.14
  451.9 1.0 fusion.13
  452.9 0.7 copy-done.4
  453.6 11.7 %cholesky.392 = f32[128,128]{1,0:T(8,128)S(1)} custom-call(f32[128,128]{1,0:T(8,128)S(1)} %cholesky.434), custom_call_target="Cholesky" | custom-call | tf_op jit(solution)/shard_map/jit(cholesky)/cholesky | solution.py:62
  465.3 9.8 %custom-call.29 = f32[1,128,128]{1,2,0:T(8,128)S(1)} custom-call(f32[1,128,128]{2,1,0:T(8,128)S(1)} %get-tuple-element.61), custom_call_target="InvertDiagBlocksLowerTriangular" | custom-call | tf_op jit(solution)/shard_map/jit(cholesky)/cholesky | solution.py:62
  475.1 1.0 constant_dynamic-update-slice_fusion.1
  476.2 1.1 convolution_subtract_fusion.4
  477.3 11.7 %cholesky.409 = f32[128,128]{1,0:T(8,128)S(1)} custom-call(f32[128,128]{1,0:T(8,128)S(1)} %convolution_subtract_fusion.4), custom_call_target="Cholesky" | custom-call | tf_op jit(solution)/shard_map/jit(cholesky)/cholesky | solution.py:62
  489.1 0.7 compare_reduce_fusion
  489.8 0.7 compare_reduce_fusion.1
  490.5 8.0 %fusion.79 = f32[256,384]{1,0:T(8,128)} fusion(f32[3072,256]{1,0:T(8,128)S(1)} %copy-done.1, f32[3072,384]{1,0:T(8,128)} %param.4), kind=kOutput, calls=%fused_computation.151 | convolution fusion | flops 3623878656 | bytes 8257536 | tf_op jit(solution)/shard_map/dot_general | solution.py:59
  499.8 1.7 select_select_fusion
  501.5 5.7 while.4
  501.5 0.6 fusion.114
  502.1 2.2 bitcast_dynamic-update-slice_fusion.5
  504.4 0.6 fusion.114
  505.0 2.2 bitcast_dynamic-update-slice_fusion.5
  507.2 0.6 copy-done.5
  507.8 20.5 %custom-call.20 = f32[2,128,128]{1,2,0:T(8,128)S(1)} custom-call(f32[2,128,128]{2,1,0:T(8,128)} %copy-done.5), custom_call_target="InvertDiagBlocksLowerTriangular" | custom-call | tf_op jit(solution)/shard_map/jit(_cho_solve)/triangular_solve | solution.py:63
  528.3 34.7 %all-reduce.8.cloned.1.call-done = f32[256,384]{1,0:T(8,128)} async-done(((f32[256,384]{1,0:T(8,128)}), f32[256,384]{1,0:T(8,128)}) %all-reduce.8.cloned.1.call-update) | async-done | bytes 393232 | tf_op jit(solution)/shard_map/psum | solution.py:60
  563.0 1.6 fusion.80
  565.0 1.2 convolution_subtract_fusion.3
  566.9 1.2 convolution_subtract_fusion.2
  568.4 8.4 %convolution_subtract_fusion = f32[3072,384]{1,0:T(8,128)} fusion(f32[3072,384]{1,0:T(8,128)} %param.4, f32[3072,256]{1,0:T(8,128)S(1)} %copy-done.1, f32[128,384]{1,0:T(8,128)S(1)} %fusion.65, f32[128,384]{1,0:T(8,128)S(1)} %fusion.64), kind=kOutput, calls=%fused_computation.4 | convolution fusion | flops 3625156608 | bytes 12976128 | tf_op jit(solution)/shard_map/dot_general | solution.py:66
  (78 shorter events, 9.6 us)
Async XLA Ops:
  6.5 281.4 %all-reduce.6.cloned.1.call-start = ((), (), s32[]{:S(2)}) async-start(), calls=%async_computation | async-start | bytes 524288 | tf_op jit(solution)/shard_map/psum | solution.py:22
  50.8 1.6 collective-permute-start
  89.6 8.8 %collective-permute-start.1 = (f32[256,256]{0,1:T(8,128)S(1)}, f32[256,256]{0,1:T(8,128)S(1)}, u32[]{:S(2)}, u32[]{:S(2)}) collective-permute-start(f32[256,256]{0,1:T(8,128)S(1)} %fusion.20), channel_id=1, source_target_pairs={{0,64},{64,0},{32,96},{96,32},{128,192},{192,128},{160,224},{224,1... | collective-permute-start | bytes 786440 | tf_op jit(solution)/shard_map/ppermute | solution.py:17
  135.5 9.3 %collective-permute-start.2 = (f32[256,256]{0,1:T(8,128)S(1)}, f32[256,256]{0,1:T(8,128)S(1)}, u32[]{:S(2)}, u32[]{:S(2)}) collective-permute-start(f32[256,256]{0,1:T(8,128)S(1)} %fusion.22), channel_id=1, source_target_pairs={{0,128},{128,0},{32,160},{160,32},{64,192},{192,64},{96,224},{224,... | collective-permute-start | bytes 786440 | tf_op jit(solution)/shard_map/ppermute | solution.py:17
  217.9 1.7 copy-start
  219.5 229.7 %all-reduce.10.cloned.1.call-start = ((), (), s32[]{:S(2)}) async-start(), calls=%async_computation.2 | async-start | bytes 6815744 | tf_op jit(solution)/shard_map/psum | solution.py:22
  289.7 273.3 %all-reduce.8.cloned.1.call-start = ((), (), s32[]{:S(2)}) async-start(), calls=%async_computation.1 | async-start | bytes 786432 | tf_op jit(solution)/shard_map/psum | solution.py:60
  449.2 41.2 %copy-start.1 = (f32[3072,256]{1,0:T(8,128)S(1)}, f32[3072,256]{1,0:T(8,128)}, u32[]{:S(2)}) copy-start(f32[3072,256]{1,0:T(8,128)} %get-tuple-element.50) | copy-start | bytes 9437188
  452.8 0.7 copy-start.4
  489.1 1.4 copy-start.3
  490.5 72.5 %copy-start.2 = (f32[256,256]{1,0:T(8,128)S(1)}, f32[256,256]{1,0:T(8,128)}, u32[]{:S(2)}) copy-start(f32[256,256]{1,0:T(8,128)} %get-tuple-element.51) | copy-start | bytes 786436
  507.2 0.6 copy-start.5
Sparse Core Ops, SparseCore 0:
  219.7 68.2 all-reduce.5
  291.6 157.5 all-reduce.9
  498.6 64.3 all-reduce.7
where the time goes:
time: 593 us; the launch traced here: 583 us
  waiting for transfers between devices  270 us (46%)
  other arithmetic  220 us (37%)
  matrix products  48.8 us (8%)
  between operations  20.2 us (3%)
  local copies, waits for them, and re-layouts  18.1 us (3%)
    psum x2, waiting for transfers between devices, broadcast(): return lax.psum(kept, axis)  226 us
    another operation x27, other arithmetic, upper_of(): return jnp.linalg.cholesky(gram).T  138 us
    another operation x7, other arithmetic, on_device(): lead_factor = jnp.linalg.cholesky(lead_gram)  34.7 us
    psum x1, waiting for transfers between devices, on_device(): projected = lax.psum(partial_proj, 'row')  34.7 us
    another operation x2, other arithmetic, on_device(): jax.scipy.linalg.cho_solve((lead_factor, True), jnp.dot(lead.T, projected...  22.2 us
    another operation x3, other arithmetic, apply_inverse(): return jax.scipy.linalg.solve_triangular(upper.T, rows.T, lower=True).T  19.7 us
  transfers between devices with their start and end apart: 6, of which 6 were waited for; matrix products, arithmetic and copies ran while one was open for 6% of the time, Pallas kernels for 0%

commit v1 on v0

--- a/solution.py
+++ b/solution.py
@@ -57,7 +57,7 @@
     vectors, lead = factor(panel)
     vectors, lead = (broadcast(vectors, "col", 0), broadcast(lead, "col", 0))
     partial_proj = lax.dot_general(vectors, matrix, (((0,), (0,)), ((), ())), precision=HIGHEST)
-    projected = lax.psum(partial_proj, "row")
+    projected = jnp.sum(lax.all_gather(partial_proj, "row"), axis=0)
     lead_gram = jnp.dot(lead.T, lead, precision=HIGHEST)
     lead_factor = jnp.linalg.cholesky(lead_gram)
     coeffs = jax.scipy.linalg.cho_solve(

time: 593 us -> 554 us (0.934)
  waiting for transfers between devices: 270 us -> 235 us
    psum x1 -> x0, waiting for transfers between devices: 34.7 us -> none  [on_device(): projected = lax.psum(partial_proj, 'row')]
  transfers between devices with their start and end apart: 6 -> 6, of which waited for: 6 -> 5; matrix products, arithmetic and copies ran while one was open for 6% -> 12% of each run, Pallas kernels for 0% -> 0%
where the time goes in v1:
time: 554 us; the launch traced here: 543 us
  waiting for transfers between devices  235 us (42%)
  other arithmetic  220 us (40%)
  matrix products  47.2 us (9%)
  between operations  20.2 us (4%)
  local copies, waits for them, and re-layouts  14.3 us (3%)
  starting transfers between devices  5.84 us (1%)
    psum x2, waiting for transfers between devices, broadcast(): return lax.psum(kept, axis)  226 us
    another operation x27, other arithmetic, upper_of(): return jnp.linalg.cholesky(gram).T  138 us
    another operation x7, other arithmetic, on_device(): lead_factor = jnp.linalg.cholesky(lead_gram)  34.7 us
    another operation x3, other arithmetic, apply_inverse(): return jax.scipy.linalg.solve_triangular(upper.T, rows.T, lower=True).T  19.7 us
    another operation x2, other arithmetic, on_device(): jax.scipy.linalg.cho_solve((lead_factor, True), jnp.dot(lead.T, projected...  19.7 us
  transfers between devices with their start and end apart: 6, of which 5 were waited for; matrix products, arithmetic and copies ran while one was open for 12% of the time, Pallas kernels for 0%

profile of v1, /device:TPU:8, one launch (start us, length us, event | category | flops | bytes accessed | tf_op | source)
XLA Modules:
  0.0 542.9 jit_solution(13848568304484892200)
XLA Ops:
  6.5 7.9 %fusion.1 = f32[256,256]{1,0:T(8,128)S(1)} fusion(f32[3072,384]{1,0:T(8,128)} %param.4), kind=kOutput, calls=%fused_computation.11 | convolution fusion | flops 2415919104 | bytes 3407872 | tf_op jit(solution)/shard_map/dot_general | solution.py:41
  14.7 11.7 %cholesky.256 = f32[128,128]{1,0:T(8,128)S(1)} custom-call(f32[128,128]{1,0:T(8,128)S(1)} %cholesky.422), custom_call_target="Cholesky" | custom-call | tf_op jit(solution)/shard_map/jit(cholesky)/cholesky | solution.py:26
  26.4 9.8 %custom-call.25 = f32[1,128,128]{1,2,0:T(8,128)S(1)} custom-call(f32[1,128,128]{2,1,0:T(8,128)S(1)} %get-tuple-element.77), custom_call_target="InvertDiagBlocksLowerTriangular" | custom-call | tf_op jit(solution)/shard_map/jit(cholesky)/cholesky | solution.py:26
  36.8 11.9 %cholesky.273 = f32[128,128]{1,0:T(8,128)S(1)} custom-call(f32[128,128]{1,0:T(8,128)S(1)} %convolution_subtract_fusion.5), custom_call_target="Cholesky" | custom-call | tf_op jit(solution)/shard_map/jit(cholesky)/cholesky | solution.py:26
  48.7 0.7 compare_reduce_fusion.8
  50.9 0.4 fusion.19
  51.3 1.1 collective-permute-done
  53.0 11.7 %cholesky.290 = f32[128,128]{1,0:T(8,128)S(1)} custom-call(f32[128,128]{1,0:T(8,128)S(1)} %cholesky.425), custom_call_target="Cholesky" | custom-call | tf_op jit(solution)/shard_map/jit(cholesky)/cholesky | solution.py:26
  64.8 9.8 %custom-call.26 = f32[1,128,128]{1,2,0:T(8,128)S(1)} custom-call(f32[1,128,128]{2,1,0:T(8,128)S(1)} %get-tuple-element.73), custom_call_target="InvertDiagBlocksLowerTriangular" | custom-call | tf_op jit(solution)/shard_map/jit(cholesky)/cholesky | solution.py:26
  75.1 11.7 %cholesky.307 = f32[128,128]{1,0:T(8,128)S(1)} custom-call(f32[128,128]{1,0:T(8,128)S(1)} %slice_subtract_fusion.2), custom_call_target="Cholesky" | custom-call | tf_op jit(solution)/shard_map/jit(cholesky)/cholesky | solution.py:26
  86.8 0.7 compare_reduce_fusion.6
  87.6 0.6 compare_reduce_fusion.7
  89.6 2.0 collective-permute-start.1
  91.6 3.8 slice_bitcast_fusion
  95.3 0.4 fusion.21
  95.7 2.7 collective-permute-done.1
  99.0 11.7 %cholesky.324 = f32[128,128]{1,0:T(8,128)S(1)} custom-call(f32[128,128]{1,0:T(8,128)S(1)} %cholesky.428), custom_call_target="Cholesky" | custom-call | tf_op jit(solution)/shard_map/jit(cholesky)/cholesky | solution.py:26
  110.8 9.8 %custom-call.27 = f32[1,128,128]{1,2,0:T(8,128)S(1)} custom-call(f32[1,128,128]{2,1,0:T(8,128)S(1)} %get-tuple-element.69), custom_call_target="InvertDiagBlocksLowerTriangular" | custom-call | tf_op jit(solution)/shard_map/jit(cholesky)/cholesky | solution.py:26
  121.1 11.7 %cholesky.341 = f32[128,128]{1,0:T(8,128)S(1)} custom-call(f32[128,128]{1,0:T(8,128)S(1)} %slice_subtract_fusion.1), custom_call_target="Cholesky" | custom-call | tf_op jit(solution)/shard_map/jit(cholesky)/cholesky | solution.py:26
  132.8 0.6 compare_reduce_fusion.4
  133.5 0.7 compare_reduce_fusion.5
  135.5 3.3 collective-permute-start.2
  138.8 0.4 fusion.23
  139.2 5.6 %collective-permute-done.2 = f32[256,256]{0,1:T(8,128)S(1)} collective-permute-done((f32[256,256]{0,1:T(8,128)S(1)}, f32[256,256]{0,1:T(8,128)S(1)}, u32[]{:S(2)}, u32[]{:S(2)}) %collective-permute-start.2) | collective-permute-done | bytes 262176 | tf_op jit(solution)/shard_map/ppermute | solution.py:17
  145.3 11.7 %cholesky.358 = f32[128,128]{1,0:T(8,128)S(1)} custom-call(f32[128,128]{1,0:T(8,128)S(1)} %cholesky.431), custom_call_target="Cholesky" | custom-call | tf_op jit(solution)/shard_map/jit(cholesky)/cholesky | solution.py:26
  157.1 9.8 %custom-call.28 = f32[1,128,128]{1,2,0:T(8,128)S(1)} custom-call(f32[1,128,128]{2,1,0:T(8,128)S(1)} %get-tuple-element.65), custom_call_target="InvertDiagBlocksLowerTriangular" | custom-call | tf_op jit(solution)/shard_map/jit(cholesky)/cholesky | solution.py:26
  167.4 11.7 %cholesky.375 = f32[128,128]{1,0:T(8,128)S(1)} custom-call(f32[128,128]{1,0:T(8,128)S(1)} %slice_subtract_fusion), custom_call_target="Cholesky" | custom-call | tf_op jit(solution)/shard_map/jit(cholesky)/cholesky | solution.py:26
  179.2 0.7 compare_reduce_fusion.2
  179.8 0.6 compare_reduce_fusion.3
  181.8 4.0 while.3
  182.0 0.6 fusion.113
  182.6 1.3 bitcast_dynamic-update-slice_fusion.4
  183.9 0.6 fusion.113
  184.5 1.3 bitcast_dynamic-update-slice_fusion.4
  185.8 19.7 %custom-call.19 = f32[2,128,128]{1,2,0:T(8,128)S(1)} custom-call(f32[2,128,128]{2,1,0:T(8,128)S(1)} %get-tuple-element.25), custom_call_target="InvertDiagBlocksLowerTriangular" | custom-call | tf_op jit(solution)/shard_map/jit(_solve_triangular)/triangular_solve | solution.py:37
  205.5 2.9 fusion.3
  208.4 5.2 convolution_subtract_fusion.1
  213.6 0.5 copy.12
  214.0 2.8 fusion.38
  217.1 0.8 slice_select_fusion
  217.9 1.7 copy-done
  219.6 1.9 broadcast_select_fusion
  221.5 66.5 %all-reduce.5.cloned.1.call-done = f32[256,256]{1,0:T(8,128)} async-done(((f32[256,256]{1,0:T(8,128)}), f32[256,256]{1,0:T(8,128)}) %all-reduce.5.cloned.1.call-update) | async-done | bytes 262160 | tf_op jit(solution)/shard_map/psum | solution.py:22
  287.9 1.7 fusion.10
  289.7 0.4 all-gather.3.cloned.1.call-start
  290.1 159.1 %all-reduce.7.cloned.1.call-done = (f32[3072,256]{1,0:T(8,128)}, f32[256,256]{1,0:T(8,128)}) async-done(((f32[3072,256]{1,0:T(8,128)}, f32[256,256]{1,0:T(8,128)}), (f32[3072,256]{1,0:T(8,128)}, f32[256,256]{1,0:T(8,128)})) %all-reduce.7.cloned.1.call-update) | async-done | bytes 3407888 | tf_op jit(solution)/shard_map/psum | solution.py:22
  449.2 9.2 %fusion.79 = f32[256,384]{1,0:T(8,128)} fusion(f32[3072,256]{1,0:T(8,128)} %get-tuple-element.50, f32[3072,384]{1,0:T(8,128)} %param.4), kind=kOutput, calls=%fused_computation.151 | convolution fusion | flops 3623878656 | bytes 8257536 | tf_op jit(solution)/shard_map/dot_general | solution.py:59
  458.5 0.6 fusion.78
  459.3 11.7 %cholesky.392 = f32[128,128]{1,0:T(8,128)S(1)} custom-call(f32[128,128]{1,0:T(8,128)S(1)} %cholesky.434), custom_call_target="Cholesky" | custom-call | tf_op jit(solution)/shard_map/jit(cholesky)/cholesky | solution.py:62
  471.1 9.9 %custom-call.29 = f32[1,128,128]{1,2,0:T(8,128)S(1)} custom-call(f32[1,128,128]{2,1,0:T(8,128)S(1)} %get-tuple-element.61), custom_call_target="InvertDiagBlocksLowerTriangular" | custom-call | tf_op jit(solution)/shard_map/jit(cholesky)/cholesky | solution.py:62
  481.5 11.7 %cholesky.409 = f32[128,128]{1,0:T(8,128)S(1)} custom-call(f32[128,128]{1,0:T(8,128)S(1)} %convolution_subtract_fusion.4), custom_call_target="Cholesky" | custom-call | tf_op jit(solution)/shard_map/jit(cholesky)/cholesky | solution.py:62
  493.3 0.7 compare_reduce_fusion
  493.9 0.6 compare_reduce_fusion.1
  495.8 3.8 while.4
  495.9 0.6 fusion.114
  496.5 1.3 bitcast_dynamic-update-slice_fusion.5
  497.8 0.6 fusion.114
  498.4 1.3 bitcast_dynamic-update-slice_fusion.5
  499.7 19.7 %custom-call.20 = f32[2,128,128]{1,2,0:T(8,128)S(1)} custom-call(f32[2,128,128]{2,1,0:T(8,128)S(1)} %get-tuple-element.33), custom_call_target="InvertDiagBlocksLowerTriangular" | custom-call | tf_op jit(solution)/shard_map/jit(_cho_solve)/triangular_solve | solution.py:63
  519.4 3.0 reduce_sum.9
  522.4 1.6 fusion.80
  524.4 1.2 convolution_subtract_fusion.3
  526.3 1.2 convolution_subtract_fusion.2
  527.8 8.4 %convolution_subtract_fusion = f32[3072,384]{1,0:T(8,128)} fusion(f32[3072,384]{1,0:T(8,128)} %param.4, f32[3072,256]{1,0:T(8,128)S(1)} %copy-done.1, f32[128,384]{1,0:T(8,128)S(1)} %fusion.65, f32[128,384]{1,0:T(8,128)S(1)} %fusion.64), kind=kOutput, calls=%fused_computation.4 | convolution fusion | flops 3625156608 | bytes 12976128 | tf_op jit(solution)/shard_map/dot_general | solution.py:66
  (75 shorter events, 6.9 us)
Async XLA Ops:
  6.5 281.4 %all-reduce.5.cloned.1.call-start = ((), (), s32[]{:S(2)}) async-start(), calls=%async_computation | async-start | bytes 524288 | tf_op jit(solution)/shard_map/psum | solution.py:22
  50.8 1.6 collective-permute-start
  89.6 8.8 %collective-permute-start.1 = (f32[256,256]{0,1:T(8,128)S(1)}, f32[256,256]{0,1:T(8,128)S(1)}, u32[]{:S(2)}, u32[]{:S(2)}) collective-permute-start(f32[256,256]{0,1:T(8,128)S(1)} %fusion.20), channel_id=1, source_target_pairs={{0,64},{64,0},{32,96},{96,32},{128,192},{192,128},{160,224},{224,1... | collective-permute-start | bytes 786440 | tf_op jit(solution)/shard_map/ppermute | solution.py:17
  135.5 9.3 %collective-permute-start.2 = (f32[256,256]{0,1:T(8,128)S(1)}, f32[256,256]{0,1:T(8,128)S(1)}, u32[]{:S(2)}, u32[]{:S(2)}) collective-permute-start(f32[256,256]{0,1:T(8,128)S(1)} %fusion.22), channel_id=1, source_target_pairs={{0,128},{128,0},{32,160},{160,32},{64,192},{192,64},{96,224},{224,... | collective-permute-start | bytes 786440 | tf_op jit(solution)/shard_map/ppermute | solution.py:17
  217.9 1.7 copy-start
  219.5 229.7 %all-reduce.7.cloned.1.call-start = ((), (), s32[]{:S(2)}) async-start(), calls=%async_computation.2 | async-start | bytes 6815744 | tf_op jit(solution)/shard_map/psum | solution.py:22
  289.7 229.7 %all-gather.3.cloned.1.call-start = ((), (), s32[]{:S(2)}) async-start(), calls=%async_computation.1 | async-start | bytes 3538944 | tf_op jit(solution)/shard_map/all_gather | solution.py:60
  449.2 9.3 %copy-start.2 = (f32[256,256]{1,0:T(8,128)S(1)}, f32[256,256]{1,0:T(8,128)}, u32[]{:S(2)}) copy-start(f32[256,256]{1,0:T(8,128)} %get-tuple-element.51) | copy-start | bytes 786436
  499.7 19.7 %copy-start.3 = (f32[256,256]{1,0:T(8,128)}, f32[256,256]{1,0:T(8,128)S(1)}, u32[]{:S(2)}) copy-start(f32[256,256]{1,0:T(8,128)S(1)} %get-tuple-element.190) | copy-start | bytes 786436
  519.4 8.4 %copy-start.1 = (f32[3072,256]{1,0:T(8,128)S(1)}, f32[3072,256]{1,0:T(8,128)}, u32[]{:S(2)}) copy-start(f32[3072,256]{1,0:T(8,128)} %get-tuple-element.50) | copy-start | bytes 9437188
Sparse Core Ops, SparseCore 0:
  219.7 68.2 all-reduce.4
  291.6 157.5 all-reduce.6
  458.6 28.7 all-gather.2
